TPU v7x, 128 devices: a whole 4x4x4 slice. The times are simulated.
128 devices in a mesh: dp: 32 (over z, y_hi, x), tensor: 4 (over y_lo, core).
Axes of the slice: x: 4, y: 4 (y_hi: 2, y_lo: 2; y = y_hi * 2 + y_lo), z: 4, core: 2. Of those that a mesh axis runs over, the one named last changes fastest.
Arguments:
- tokens: bfloat16 [32, 4, 128, 2048], P('dp', 'tensor'), may hold values from -6 to 6
- doc_ids: int32 [32, 4, 128], P('dp'), may hold values from 0 to 3, never falling along the last dimension, each value on 1 to 64 neighbouring positions
- attn_gain: float32 [2048], P(('dp', 'tensor')), may hold values from 0.5 to 1.5
- forget_floor: float32 [2048], P(('dp', 'tensor')), may hold values from 0.5 to 0.98
- w_query: bfloat16 [2048, 2048], P('dp', 'tensor'), may hold values from -0.125 to 0.125
- w_forget: bfloat16 [2048, 2048], P('dp', 'tensor'), may hold values from -0.125 to 0.125
- w_value: bfloat16 [2048, 2048], P('dp', 'tensor'), may hold values from -0.125 to 0.125
- w_outgate: bfloat16 [2048, 2048], P('dp', 'tensor'), may hold values from -0.125 to 0.125
- w_output: bfloat16 [2048, 2048], P('tensor', 'dp'), may hold values from -0.125 to 0.125
- mlp_gain: float32 [2048], P(('dp', 'tensor')), may hold values from 0.5 to 1.5
- w_gate: bfloat16 [2048, 5632], P('dp', 'tensor'), may hold values from -0.125 to 0.125
- w_up: bfloat16 [2048, 5632], P('dp', 'tensor'), may hold values from -0.125 to 0.125
- w_down: bfloat16 [5632, 2048], P('tensor', 'dp'), may hold values from -0.078125 to 0.078125
- cotangent: bfloat16 [32, 4, 128, 2048], P('dp', 'tensor'), may hold values from -6 to 6
Outputs:
- layer_out: bfloat16 [32, 4, 128, 2048], P('dp', 'tensor')
- grad_tokens: float32 [32, 4, 128, 2048], P('dp', 'tensor')
- grad_attn_gain: float32 [2048], P(('dp', 'tensor'))
- grad_floor: float32 [2048], P(('dp', 'tensor'))
- grad_query: float32 [2048, 2048], P('dp', 'tensor')
- grad_forget: float32 [2048, 2048], P('dp', 'tensor')
- grad_value: float32 [2048, 2048], P('dp', 'tensor')
- grad_outgate: float32 [2048, 2048], P('dp', 'tensor')
- grad_output: float32 [2048, 2048], P('tensor', 'dp')
- grad_mlp_gain: float32 [2048], P(('dp', 'tensor'))
- grad_gate: float32 [2048, 5632], P('dp', 'tensor')
- grad_up: float32 [2048, 5632], P('dp', 'tensor')
- grad_down: float32 [5632, 2048], P('tensor', 'dp')
Inputs may be any that keep to these rules, and one draw needn't show every extreme that they name: `doc_ids`: within each row of 128 tokens the sequence numbers never fall; each sequence has 1 to 64 tokens, and the longest has exactly 64.
All inputs are finite; a program needn't handle non-finite values.
Results may differ from a plain program's by a relative error of at most 0.025.
Values may be sent and summed in bfloat16 or wider, within the bound.
No kernel may reach another device: no remote copies, remote signals or barrier semaphores. Data moves between devices by JAX's collectives and lax.ppermute only.
A program may use at most 192 MiB of HBM per device.

v0:
```python
import jax
import jax.numpy as jnp
from jax import lax
from jax.sharding import PartitionSpec as P

HK = 128
HIGHEST = lax.Precision.HIGHEST
epsilon = 1e-06


def row_scale(values):
    return lax.rsqrt(jnp.mean(values * values, axis=-1, keepdims=True) + epsilon)


def silu_slope(values):
    sigmoid_val = jax.nn.sigmoid(values)
    return sigmoid_val * (1.0 + values * (1.0 - sigmoid_val))


def matmul_plain(left, right):
    return jnp.dot(left, right, preferred_element_type=jnp.float32)


def times_trans(left, right):
    return lax.dot_general(
        left, right, (((1,), (1,)), ((), ())), preferred_element_type=jnp.float32
    )


def trans_times(left, right):
    return lax.dot_general(
        left, right, (((0,), (0,)), ((), ())), preferred_element_type=jnp.float32
    )


def recurrence(query, forget_raw, value, floor_vec, doc_rows):
    length = query.shape[1]
    forget = floor_vec + (1.0 - floor_vec) * jax.nn.sigmoid(forget_raw)
    log_forget = jnp.log(forget)
    keyed = 1.0 - forget
    position = jnp.arange(length)
    same_doc = doc_rows[:, :, None] == doc_rows[:, None, :]
    causal = same_doc & (position[:, None] >= position[None, :])
    starts = jnp.concatenate(
        [jnp.zeros_like(doc_rows[:, :1], dtype=bool), doc_rows[:, 1:] == doc_rows[:, :-1]], axis=1
    )
    summing = (causal & starts[:, None, :]).astype(jnp.float32)
    running = jnp.einsum("rij,rjhk->rihk", summing, log_forget, precision=HIGHEST)
    query_t = query * jnp.exp(running)
    key_t = keyed * jnp.exp(-running)
    scores = jnp.einsum("rihk,rjhk->rhij", query_t, key_t, precision=HIGHEST)
    scores = jnp.where(causal[:, None], scores, 0.0)
    return jnp.einsum("rhij,rjhv->rihv", scores, value, precision=HIGHEST)


ON_CHIP = [(0, 1), (1, 0), (2, 3), (3, 2)]
ACROSS = [(0, 2), (2, 0), (1, 3), (3, 1)]
SLOT_XOR = (0, 2, 1, 3)


def row_gather(values):
    across = lax.ppermute(values, "tensor", ACROSS)
    pair = jnp.stack([values, across])
    other = lax.ppermute(pair, "tensor", ON_CHIP)
    return jnp.concatenate([pair, other]).reshape((-1,) + values.shape[1:])


def row_sum(values):
    blocks = values.reshape((4, -1) + values.shape[1:])
    got = lax.ppermute(blocks[2:], "tensor", ON_CHIP)
    mine = blocks[0] + got[0]
    theirs = blocks[1] + got[1]
    return mine + lax.ppermute(theirs, "tensor", ACROSS)


def spread_sum(values, axis, count):
    blocks = values.reshape((count, -1) + values.shape[1:])
    got = lax.all_to_all(blocks, axis, 0, 0, tiled=False)
    return got.astype(jnp.float32).sum(axis=0)


def small_gather(vectors):
    count = 128
    spread = jnp.broadcast_to(vectors[None], (count,) + vectors.shape)
    got = lax.all_to_all(spread, ("dp", "tensor"), 0, 0, tiled=False)
    return jnp.swapaxes(got, 0, 1).reshape(vectors.shape[0], -1)


def small_sum(vectors):
    count = 128
    blocks = vectors.reshape(vectors.shape[0], count, -1)
    got = lax.all_to_all(jnp.swapaxes(blocks, 0, 1), ("dp", "tensor"), 0, 0, tiled=False)
    return got.sum(axis=0)


def shards(
    tokens,
    doc_ids,
    attn_gain,
    forget_floor,
    w_query,
    w_forget,
    w_value,
    w_outgate,
    w_output,
    mlp_gain,
    w_gate,
    w_up,
    w_down,
    cotangent,
):
    gains = small_gather(jnp.stack([attn_gain, forget_floor, mlp_gain]))
    attn_full, floor_full, mlp_full = (gains[0], gains[1], gains[2])
    part_index = lax.axis_index("tensor")
    local_width = w_query.shape[1]
    local_heads = local_width // HK
    hidden_width = w_gate.shape[1]
    floor_local = lax.dynamic_slice_in_dim(
        floor_full, part_index * local_width, local_width
    ).reshape(local_heads, HK)
    model_width = attn_full.shape[0]
    slot_rows = jnp.bitwise_xor(part_index, jnp.array(SLOT_XOR, jnp.int32))
    doc_all = jnp.take(doc_ids[0], slot_rows, axis=0)
    row_count = doc_all.shape[0]
    resid_in = tokens[0].reshape(-1, model_width).astype(jnp.float32)
    cot_local = cotangent[0].reshape(-1, model_width)
    attn_pack = jnp.concatenate([w_query, w_forget, w_value, w_outgate, w_output.T], axis=1)
    mlp_pack = jnp.concatenate([w_gate, w_up, w_down.T], axis=1)
    attn_all = lax.all_gather(attn_pack, "dp", axis=0, tiled=True)
    mlp_all = lax.all_gather(mlp_pack, "dp", axis=0, tiled=True)
    wq_all = attn_all[:, 0 * local_width : 1 * local_width]
    wf_all = attn_all[:, 1 * local_width : 2 * local_width]
    wv_all = attn_all[:, 2 * local_width : 3 * local_width]
    wg_all = attn_all[:, 3 * local_width : 4 * local_width]
    wo_t = attn_all[:, 4 * local_width : 5 * local_width]
    wgate_all = mlp_all[:, 0:hidden_width]
    wup_all = mlp_all[:, hidden_width : 2 * hidden_width]
    wdown_t = mlp_all[:, 2 * hidden_width : 3 * hidden_width]
    scale_one = row_scale(resid_in)
    normed = row_gather((resid_in * scale_one * attn_full).astype(jnp.bfloat16))
    query = matmul_plain(normed, wq_all)
    forget_raw = matmul_plain(normed, wf_all)
    value = matmul_plain(normed, wv_all)
    out_gate = matmul_plain(normed, wg_all)

    def mixer(query_in, forget_in, value_in, floor_in):

        def shaped(arr):
            return arr.reshape(row_count, -1, local_heads, HK)

        mixed_rows = recurrence(
            shaped(query_in), shaped(forget_in), shaped(value_in), floor_in, doc_all
        )
        return mixed_rows.reshape(query_in.shape[0], local_width)

    mixed, pullback = jax.vjp(mixer, query, forget_raw, value, floor_local)
    gate_act = jax.nn.silu(out_gate)
    gated = (mixed * gate_act).astype(jnp.bfloat16)
    branch = row_sum(times_trans(gated, wo_t))
    resid = resid_in + branch
    scale_two = row_scale(resid)
    normed2 = row_gather((resid * scale_two * mlp_full).astype(jnp.bfloat16))
    gate_proj = matmul_plain(normed2, wgate_all)
    up_proj = matmul_plain(normed2, wup_all)
    gate_silu = jax.nn.silu(gate_proj)
    hidden = (gate_silu * up_proj).astype(jnp.bfloat16)
    ffn_out = row_sum(times_trans(hidden, wdown_t))
    layer_out = (resid + ffn_out).astype(jnp.bfloat16).reshape(tokens.shape)
    cot_full = row_gather(cot_local)
    d_hidden = matmul_plain(cot_full, wdown_t)
    grad_down_t = trans_times(cot_full, hidden)
    d_gate = (d_hidden * up_proj * silu_slope(gate_proj)).astype(jnp.bfloat16)
    d_up = (d_hidden * gate_silu).astype(jnp.bfloat16)
    grad_gate = trans_times(normed2, d_gate)
    grad_up = trans_times(normed2, d_up)
    mlp_grads = jnp.concatenate(
        [
            grad_gate.astype(jnp.bfloat16),
            grad_up.astype(jnp.bfloat16),
            grad_down_t.astype(jnp.bfloat16),
        ],
        axis=1,
    )
    mlp_red = lax.psum_scatter(mlp_grads, "dp", scatter_dimension=0, tiled=True).astype(jnp.float32)
    d_normed2 = row_sum(times_trans(d_gate, wgate_all) + times_trans(d_up, wup_all))
    grad_mlp = jnp.sum(d_normed2 * resid * scale_two, axis=0)
    inner_two = jnp.mean(d_normed2 * mlp_full * resid, axis=-1, keepdims=True)
    d_resid = (
        cot_local.astype(jnp.float32)
        + d_normed2 * mlp_full * scale_two
        - resid * scale_two**3 * inner_two
    )
    d_branch = row_gather(d_resid.astype(jnp.bfloat16))
    d_gated = matmul_plain(d_branch, wo_t)
    grad_output_t = trans_times(d_branch, gated)
    d_mixed = d_gated * gate_act
    d_outgate = (d_gated * mixed * silu_slope(out_gate)).astype(jnp.bfloat16)
    d_query, d_forget, d_value, d_floor = pullback(d_mixed)
    d_query = d_query.astype(jnp.bfloat16)
    d_forget = d_forget.astype(jnp.bfloat16)
    d_value = d_value.astype(jnp.bfloat16)
    grad_query = trans_times(normed, d_query)
    grad_forget = trans_times(normed, d_forget)
    grad_value = trans_times(normed, d_value)
    grad_outgate = trans_times(normed, d_outgate)
    attn_grads = jnp.concatenate(
        [
            grad_query.astype(jnp.bfloat16),
            grad_forget.astype(jnp.bfloat16),
            grad_value.astype(jnp.bfloat16),
            grad_outgate.astype(jnp.bfloat16),
            grad_output_t.astype(jnp.bfloat16),
        ],
        axis=1,
    )
    attn_red = spread_sum(attn_grads, "dp", 32)
    d_normed = row_sum(
        times_trans(d_query, wq_all)
        + times_trans(d_forget, wf_all)
        + times_trans(d_value, wv_all)
        + times_trans(d_outgate, wg_all)
    )
    grad_attn = jnp.sum(d_normed * resid_in * scale_one, axis=0)
    inner_one = jnp.mean(d_normed * attn_full * resid_in, axis=-1, keepdims=True)
    grad_tokens = (
        d_resid + d_normed * attn_full * scale_one - resid_in * scale_one**3 * inner_one
    ).reshape(tokens.shape)
    floor_vector = lax.dynamic_update_slice(
        jnp.zeros((model_width,), jnp.float32), d_floor.reshape(-1), (part_index * local_width,)
    )
    reduced_small = small_sum(jnp.stack([grad_attn, floor_vector, grad_mlp]))
    return (
        layer_out,
        grad_tokens,
        reduced_small[0],
        reduced_small[1],
        attn_red[:, 0 * local_width : 1 * local_width],
        attn_red[:, 1 * local_width : 2 * local_width],
        attn_red[:, 2 * local_width : 3 * local_width],
        attn_red[:, 3 * local_width : 4 * local_width],
        attn_red[:, 4 * local_width : 5 * local_width].T,
        reduced_small[2],
        mlp_red[:, 0:hidden_width],
        mlp_red[:, hidden_width : 2 * hidden_width],
        mlp_red[:, 2 * hidden_width : 3 * hidden_width].T,
    )


def solution(mesh):
    return jax.shard_map(
        shards,
        mesh=mesh,
        in_specs=(
            P("dp", "tensor", None, None),
            P("dp", None, None),
            P(("dp", "tensor")),
            P(("dp", "tensor")),
            P("dp", "tensor"),
            P("dp", "tensor"),
            P("dp", "tensor"),
            P("dp", "tensor"),
            P("tensor", "dp"),
            P(("dp", "tensor")),
            P("dp", "tensor"),
            P("dp", "tensor"),
            P("tensor", "dp"),
            P("dp", "tensor", None, None),
        ),
        out_specs=(
            P("dp", "tensor", None, None),
            P("dp", "tensor", None, None),
            P(("dp", "tensor")),
            P(("dp", "tensor")),
            P("dp", "tensor"),
            P("dp", "tensor"),
            P("dp", "tensor"),
            P("dp", "tensor"),
            P("tensor", "dp"),
            P(("dp", "tensor")),
            P("dp", "tensor"),
            P("dp", "tensor"),
            P("tensor", "dp"),
        ),
        check_vma=False,
    )
```

profile of v0, /device:TPU:0, one launch (start us, length us, event | category | flops | bytes accessed | tf_op | source)
XLA Modules:
  0.0 807.6 jit_solution(461497468060412222)
XLA Ops:
  15.1 11.1 %all-to-all-start = ((f32[128,3,16]{2,1,0:T(4,128)}), f32[128,3,16]{2,1,0:T(4,128)S(1)}, u32[]{:S(2)}, u32[]{:S(2)}) async-start(f32[128,3,16]{2,1,0:T(4,128)} %broadcast_in_dim.29), calls=%async_computation | async-start | bytes 524288 | tf_op jit(solution)/shard_map/all_to_all | solution.py:85
  27.1 11.5 %all-to-all-done = f32[128,3,16]{2,1,0:T(4,128)S(1)} async-done(((f32[128,3,16]{2,1,0:T(4,128)}), f32[128,3,16]{2,1,0:T(4,128)S(1)}, u32[]{:S(2)}, u32[]{:S(2)}) %all-to-all-start) | async-done | bytes 24608 | tf_op jit(solution)/shard_map/all_to_all | solution.py:85
  40.2 15.4 %collective-permute-done = bf16[128,2048]{1,0:T(8,128)(2,1)S(1)} collective-permute-done((bf16[128,2048]{1,0:T(8,128)(2,1)S(1)}, bf16[128,2048]{1,0:T(8,128)(2,1)S(1)}, u32[]{:S(2)}, u32[]{:S(2)}) %collective-permute-start) | collective-permute-done | bytes 524320 | tf_op jit(solution)/shard_map/ppermute | solution.py:62
  58.6 2.8 pad_maximum_fusion.1
  61.4 72.5 %all-gather.3.cloned.1.call-done = bf16[2048,2560]{1,0:T(8,128)(2,1)} async-done(((bf16[64,2560]{1,0:T(8,128)(2,1)}), bf16[2048,2560]{1,0:T(8,128)(2,1)}) %all-gather.3.cloned.1.call-update) | async-done | bytes 10485776 | tf_op jit(solution)/shard_map/all_gather | solution.py:129
  133.9 5.3 slice_bitcast_fusion
  139.2 4.1 copy.78
  143.3 4.1 copy.80
  149.8 3.6 fusion.56
  160.5 2.9 fusion.25
  167.5 5.4 fusion.74
  172.9 3.1 fusion.29
  176.4 4.1 collective-permute-done.2
  182.8 26.3 %collective-permute-done.3 = f32[128,2048]{1,0:T(8,128)} collective-permute-done((f32[128,2048]{1,0:T(8,128)S(1)}, f32[128,2048]{1,0:T(8,128)}, u32[]{:S(2)}, u32[]{:S(2)}) %collective-permute-start.3) | collective-permute-done | bytes 1048608 | tf_op jit(solution)/shard_map/ppermute | solution.py:73
  211.9 13.1 %collective-permute-done.8 = bf16[128,2048]{1,0:T(8,128)(2,1)} collective-permute-done((bf16[128,2048]{1,0:T(8,128)(2,1)S(1)}, bf16[128,2048]{1,0:T(8,128)(2,1)}, u32[]{:S(2)}, u32[]{:S(2)}) %collective-permute-start.8) | collective-permute-done | bytes 524320 | tf_op jit(solution)/shard_map/ppermute | solution.py:62
  226.3 20.7 %collective-permute-done.4 = bf16[128,2048]{1,0:T(8,128)(2,1)S(1)} collective-permute-done((bf16[128,2048]{1,0:T(8,128)(2,1)S(1)}, bf16[128,2048]{1,0:T(8,128)(2,1)S(1)}, u32[]{:S(2)}, u32[]{:S(2)}) %collective-permute-start.4) | collective-permute-done | bytes 524320 | tf_op jit(solution)/shard_map/ppermute | solution.py:62
  251.4 63.5 %all-gather.5.cloned.1.call-done = bf16[2048,4224]{1,0:T(8,128)(2,1)} async-done(((bf16[64,4224]{1,0:T(8,128)(2,1)}), bf16[2048,4224]{1,0:T(8,128)(2,1)}) %all-gather.5.cloned.1.call-update) | async-done | bytes 17301520 | tf_op jit(solution)/shard_map/all_gather | solution.py:130
  315.0 7.0 fusion
  323.9 3.4 fusion.6
  327.3 7.3 multiply_convert_fusion.1
  334.7 3.5 convolution_convert_fusion
  338.2 3.5 convolution_convert_fusion.1
  341.6 3.5 convolution_convert_fusion.2
  345.1 7.9 pad_maximum_fusion
  353.0 21.9 %copy.106 = bf16[2048,4224]{1,0:T(8,128)(2,1)} copy(bf16[2048,4224]{0,1:T(8,128)(2,1)} %pad_maximum_fusion) | data formatting | bytes 34603008
  374.9 6.0 fusion.4
  381.0 5.6 fusion.12
  387.9 5.5 fusion.2
  394.5 3.4 collective-permute-done.6
  398.6 29.0 %collective-permute-done.11 = f32[128,2048]{1,0:T(8,128)S(1)} collective-permute-done((f32[128,2048]{1,0:T(8,128)S(1)}, f32[128,2048]{1,0:T(8,128)S(1)}, u32[]{:S(2)}, u32[]{:S(2)}) %collective-permute-start.11) | collective-permute-done | bytes 1048608 | tf_op jit(solution)/shard_map/ppermute | solution.py:73
  428.1 29.3 %collective-permute-done.7 = f32[128,2048]{1,0:T(8,128)S(1)} collective-permute-done((f32[128,2048]{1,0:T(8,128)S(1)}, f32[128,2048]{1,0:T(8,128)S(1)}, u32[]{:S(2)}, u32[]{:S(2)}) %collective-permute-start.7) | collective-permute-done | bytes 1048608 | tf_op jit(solution)/shard_map/ppermute | solution.py:73
  459.6 17.0 %collective-permute-done.12 = bf16[128,2048]{1,0:T(8,128)(2,1)S(1)} collective-permute-done((bf16[128,2048]{1,0:T(8,128)(2,1)S(1)}, bf16[128,2048]{1,0:T(8,128)(2,1)S(1)}, u32[]{:S(2)}, u32[]{:S(2)}) %collective-permute-start.12) | collective-permute-done | bytes 524320 | tf_op jit(solution)/shard_map/ppermute | solution.py:62
  477.1 2.6 collective-permute-done.13
  480.0 4.7 fusion.76
  487.6 3.2 fusion.59
  492.1 3.3 convolution_select_fusion
  510.0 4.2 fusion.19
  518.6 4.4 fusion.18
  523.0 2.7 fusion.17
  525.7 2.7 fusion.16
  528.4 21.0 %collective-permute-done.15 = f32[128,2048]{1,0:T(8,128)} collective-permute-done((f32[128,2048]{1,0:T(8,128)S(1)}, f32[128,2048]{1,0:T(8,128)}, u32[]{:S(2)}, u32[]{:S(2)}) %collective-permute-start.15) | collective-permute-done | bytes 1048608 | tf_op jit(solution)/shard_map/ppermute | solution.py:73
  552.6 7.2 all-to-all-start.1
  559.8 4.2 fusion.15
  564.0 13.9 %copy.92 = bf16[2048,2560]{1,0:T(8,128)(2,1)} copy(bf16[2048,2560]{0,1:T(8,128)(2,1)} %fusion.15) | data formatting | bytes 20971520 | tf_op jit(solution)/shard_map/concatenate | solution.py:206
  578.0 9.8 %all-to-all-start.2 = ((bf16[32,64,2560]{2,1,0:T(8,128)(2,1)}), bf16[32,64,2560]{2,1,0:T(8,128)(2,1)}, u32[]{:S(2)}, u32[]{:S(2)}) async-start(bf16[32,64,2560]{2,1,0:T(8,128)(2,1)} %bitcast.265), calls=%async_computation.2 | async-start | bytes 20971520 | tf_op jit(solution)/shard_map/all_to_all | solution.py:78
  589.7 163.9 %all-to-all-done.2 = bf16[32,64,2560]{2,1,0:T(8,128)(2,1)} async-done(((bf16[32,64,2560]{2,1,0:T(8,128)(2,1)}), bf16[32,64,2560]{2,1,0:T(8,128)(2,1)}, u32[]{:S(2)}, u32[]{:S(2)}) %all-to-all-start.2) | async-done | bytes 10485792 | tf_op jit(solution)/shard_map/all_to_all | solution.py:78
  753.7 5.8 convert_reduce_fusion
  760.3 31.9 %reduce-scatter.4.cloned.1.call-done = bf16[64,4224]{1,0:T(8,128)(2,1)} async-done(((bf16[2048,4224]{1,0:T(8,128)(2,1)}), bf16[64,4224]{1,0:T(8,128)(2,1)}) %reduce-scatter.4.cloned.1.call-update) | async-done | bytes 540688
  (210 shorter events, 83.6 us)
Async XLA Ops:
  7.2 48.7 %copy-start = (s32[1,4,128]{2,1,0:T(4,128)S(1)}, s32[1,4,128]{2,1,0:T(4,128)}, u32[]{:S(2)}) copy-start(s32[1,4,128]{2,1,0:T(4,128)} %param.16) | copy-start | bytes 6148
  7.2 7.2 copy-start.32
  7.2 7.2 copy-start.33
  7.2 7.2 copy-start.34
  7.2 19.1 %copy-start.3 = (bf16[1,1,128,2048]{3,2,1,0:T(8,128)(2,1)S(1)}, bf16[1,1,128,2048]{3,2,1,0:T(8,128)(2,1)}, u32[]{:S(2)}) copy-start(bf16[1,1,128,2048]{3,2,1,0:T(8,128)(2,1)} %param.15) | copy-start | bytes 1572868
  7.2 126.6 %all-gather.3.cloned.1.call-start = ((), (), s32[]{:S(2)}) async-start(), calls=%async_computation.4 | async-start | bytes 10813440 | tf_op jit(solution)/shard_map/all_gather | solution.py:129
  12.3 302.7 %all-gather.5.cloned.1.call-start = ((), (), s32[]{:S(2)}) async-start(), calls=%async_computation.5 | async-start | bytes 17842176 | tf_op jit(solution)/shard_map/all_gather | solution.py:130
  15.1 23.4 %all-to-all-start = ((f32[128,3,16]{2,1,0:T(4,128)}), f32[128,3,16]{2,1,0:T(4,128)S(1)}, u32[]{:S(2)}, u32[]{:S(2)}) async-start(f32[128,3,16]{2,1,0:T(4,128)} %broadcast_in_dim.29), calls=%async_computation | async-start | bytes 524288 | tf_op jit(solution)/shard_map/all_to_all | solution.py:85
  26.3 765.9 %reduce-scatter.4.cloned.1.call-start = ((), (), s32[]{:S(2)}) async-start(), calls=%async_computation.6 | async-start | bytes 17842176
  27.1 28.7 %copy-start.29 = (f32[128]{0:T(128)}, f32[128]{0:T(128)S(1)}, u32[]{:S(2)}) copy-start(f32[128]{0:T(128)S(1)} %get-tuple-element.105) | copy-start | bytes 1540
  39.2 16.6 %copy-start.27 = (f32[2048]{0:T(1024)}, f32[2048]{0:T(1024)S(1)}, u32[]{:S(2)}) copy-start(f32[2048]{0:T(1024)S(1)} %mul.250) | copy-start | bytes 24580
  39.2 16.7 %copy-start.35 = (s32[4]{0:T(128)S(1)}, s32[4]{0:T(128)}, u32[]{:S(2)}) copy-start(s32[4]{0:T(128)} %constant.52.clone) | copy-start | bytes 52
  39.4 16.3 %collective-permute-start = (bf16[128,2048]{1,0:T(8,128)(2,1)S(1)}, bf16[128,2048]{1,0:T(8,128)(2,1)S(1)}, u32[]{:S(2)}, u32[]{:S(2)}) collective-permute-start(bf16[128,2048]{1,0:T(8,128)(2,1)S(1)} %fusion.62), channel_id=1, source_target_pairs={{0,2},{2,0},{1,3},{3,1},{4,6},{6,4},{5,7},{7,5},{8,10},{10,8},{9,1... | collective-permute-start | bytes 1572872 | tf_op jit(solution)/shard_map/ppermute | solution.py:62
  55.7 5.8 copy-start.20
  55.8 2.9 collective-permute-start.1
  149.8 4.5 copy-start.21
  153.4 4.6 copy-start.6
  176.3 5.6 copy-start.8
  176.3 4.2 collective-permute-start.2
  180.7 28.5 %collective-permute-start.3 = (f32[128,2048]{1,0:T(8,128)S(1)}, f32[128,2048]{1,0:T(8,128)}, u32[]{:S(2)}, u32[]{:S(2)}) collective-permute-start(f32[128,2048]{1,0:T(8,128)S(1)} %fusion.88), channel_id=1, source_target_pairs={{0,2},{2,0},{1,3},{3,1},{4,6},{6,4},{5,7},{7,5},{8,10},{10,8},{9,1... | collective-permute-start | bytes 3145736 | tf_op jit(solution)/shard_map/ppermute | solution.py:73
  181.9 43.1 %collective-permute-start.8 = (bf16[128,2048]{1,0:T(8,128)(2,1)S(1)}, bf16[128,2048]{1,0:T(8,128)(2,1)}, u32[]{:S(2)}, u32[]{:S(2)}) collective-permute-start(bf16[128,2048]{1,0:T(8,128)(2,1)S(1)} %bitcast.268), channel_id=1, source_target_pairs={{0,2},{2,0},{1,3},{3,1},{4,6},{6,4},{5,7},{7,5},{8,10},{10,8},{9,1... | collective-permute-start | bytes 1572872 | tf_op jit(solution)/shard_map/ppermute | solution.py:62
  211.6 35.5 %collective-permute-start.4 = (bf16[128,2048]{1,0:T(8,128)(2,1)S(1)}, bf16[128,2048]{1,0:T(8,128)(2,1)S(1)}, u32[]{:S(2)}, u32[]{:S(2)}) collective-permute-start(bf16[128,2048]{1,0:T(8,128)(2,1)S(1)} %multiply_convert_fusion.4), channel_id=1, source_target_pairs={{0,2},{2,0},{1,3},{3,1},{4,6},{6,4},{5,7},{7,5},{8,10},{10,8},{9,1... | collective-permute-start | bytes 1572872 | tf_op jit(solution)/shard_map/ppermute | solution.py:62
  226.1 21.1 %collective-permute-start.9 = (bf16[2,128,2048]{2,1,0:T(8,128)(2,1)S(1)}, bf16[2,128,2048]{2,1,0:T(8,128)(2,1)S(1)}, u32[]{:S(2)}, u32[]{:S(2)}) collective-permute-start(bf16[2,128,2048]{2,1,0:T(8,128)(2,1)S(1)} %pad_maximum_fusion.7), channel_id=1, source_target_pairs={{0,1},{1,0},{2,3},{3,2},{4,5},{5,4},{6,7},{7,6},{8,9},{9,8},{10,11... | collective-permute-start | bytes 3145736 | tf_op jit(solution)/shard_map/ppermute | solution.py:64
  247.1 2.7 collective-permute-start.5
  315.0 7.0 copy-start.17
  315.0 8.9 %copy-start.36 = (bf16[2048,4224]{1,0:T(8,128)(2,1)S(1)}, bf16[2048,4224]{1,0:T(8,128)(2,1)}, u32[]{:S(2)}) copy-start(bf16[2048,4224]{1,0:T(8,128)(2,1)} %all-gather.5.cloned.1.call-done) | copy-start | bytes 51904516
  327.3 7.4 copy-start.16
  334.7 7.0 copy-start.37
  374.9 6.0 copy-start.38
  386.8 6.9 collective-permute-start.10
  393.6 4.2 collective-permute-start.6
  393.8 33.8 %collective-permute-start.11 = (f32[128,2048]{1,0:T(8,128)S(1)}, f32[128,2048]{1,0:T(8,128)S(1)}, u32[]{:S(2)}, u32[]{:S(2)}) collective-permute-start(f32[128,2048]{1,0:T(8,128)S(1)} %fusion.80), channel_id=1, source_target_pairs={{0,2},{2,0},{1,3},{3,1},{4,6},{6,4},{5,7},{7,5},{8,10},{10,8},{9,1... | collective-permute-start | bytes 3145736 | tf_op jit(solution)/shard_map/ppermute | solution.py:73
  398.0 59.4 %collective-permute-start.7 = (f32[128,2048]{1,0:T(8,128)S(1)}, f32[128,2048]{1,0:T(8,128)S(1)}, u32[]{:S(2)}, u32[]{:S(2)}) collective-permute-start(f32[128,2048]{1,0:T(8,128)S(1)} %fusion.83), channel_id=1, source_target_pairs={{0,2},{2,0},{1,3},{3,1},{4,6},{6,4},{5,7},{7,5},{8,10},{10,8},{9,1... | collective-permute-start | bytes 3145736 | tf_op jit(solution)/shard_map/ppermute | solution.py:73
  459.1 17.6 %collective-permute-start.12 = (bf16[128,2048]{1,0:T(8,128)(2,1)S(1)}, bf16[128,2048]{1,0:T(8,128)(2,1)S(1)}, u32[]{:S(2)}, u32[]{:S(2)}) collective-permute-start(bf16[128,2048]{1,0:T(8,128)(2,1)S(1)} %get-tuple-element.75), channel_id=1, source_target_pairs={{0,2},{2,0},{1,3},{3,1},{4,6},{6,4},{5,7},{7,5},{8,10},{10,8},{9,1... | collective-permute-start | bytes 1572872 | tf_op jit(solution)/shard_map/ppermute | solution.py:62
  476.8 3.0 collective-permute-start.13
  479.9 4.8 copy-start.15
  495.5 6.5 slice-start
  497.4 4.5 slice-start.1
  509.9 4.5 collective-permute-start.14
  516.1 33.3 %collective-permute-start.15 = (f32[128,2048]{1,0:T(8,128)S(1)}, f32[128,2048]{1,0:T(8,128)}, u32[]{:S(2)}, u32[]{:S(2)}) collective-permute-start(f32[128,2048]{1,0:T(8,128)S(1)} %fusion.77), channel_id=1, source_target_pairs={{0,2},{2,0},{1,3},{3,1},{4,6},{6,4},{5,7},{7,5},{8,10},{10,8},{9,1... | collective-permute-start | bytes 3145736 | tf_op jit(solution)/shard_map/ppermute | solution.py:73
  525.7 23.7 %copy-start.28 = (f32[2048]{0:T(1024)S(1)}, f32[2048]{0:T(1024)}, u32[]{:S(2)}) copy-start(f32[2048]{0:T(1024)} %copy-done.27) | copy-start | bytes 24580
  525.7 23.7 %copy-start.30 = (f32[128]{0:T(128)S(1)}, f32[128]{0:T(128)}, u32[]{:S(2)}) copy-start(f32[128]{0:T(128)} %copy-done.29) | copy-start | bytes 1540
  528.4 31.4 %copy-start.23 = (bf16[512,512]{1,0:T(8,128)(2,1)S(1)}, bf16[512,512]{1,0:T(8,128)(2,1)}, u32[]{:S(2)}) copy-start(bf16[512,512]{1,0:T(8,128)(2,1)} %copy-done.22) | copy-start | bytes 1572868
  552.6 25.4 %all-to-all-start.1 = ((f32[128,3,16]{2,1,0:T(4,128)}), f32[128,3,16]{2,1,0:T(4,128)S(1)}, u32[]{:S(2)}, u32[]{:S(2)}) async-start(f32[128,3,16]{2,1,0:T(4,128)} %copy.91), calls=%async_computation.1 | async-start | bytes 524288 | tf_op jit(solution)/shard_map/all_to_all | solution.py:92
  577.9 9.8 %copy-start.10 = (f32[128,2048]{1,0:T(8,128)S(1)}, f32[128,2048]{1,0:T(8,128)}, u32[]{:S(2)}) copy-start(f32[128,2048]{1,0:T(8,128)} %get-tuple-element.76) | copy-start | bytes 3145732
  578.0 9.8 %copy-start.31 = (f32[128]{0:T(128)S(1)}, f32[128]{0:T(128)}, u32[]{:S(2)}) copy-start(f32[128]{0:T(128)} %get-tuple-element.104) | copy-start | bytes 1540
  578.0 175.7 %all-to-all-start.2 = ((bf16[32,64,2560]{2,1,0:T(8,128)(2,1)}), bf16[32,64,2560]{2,1,0:T(8,128)(2,1)}, u32[]{:S(2)}, u32[]{:S(2)}) async-start(bf16[32,64,2560]{2,1,0:T(8,128)(2,1)} %bitcast.265), calls=%async_computation.2 | async-start | bytes 20971520 | tf_op jit(solution)/shard_map/all_to_all | solution.py:78
  795.3 5.3 copy-start.1
  (20 other events, 51.6 us)
Sparse Core Ops, SparseCore 0:
  12.4 121.4 all-gather.2
  136.9 177.9 all-gather.4
  375.0 417.0 reduce-scatter.3
where the time goes:
time: 813 us; the launch traced here: 808 us
  waiting for transfers between devices  527 us (65%)
  matrix products  108 us (13%)
  local copies, waits for them, and re-layouts  86.1 us (11%)
  other arithmetic  37 us (5%)
  starting transfers between devices  34 us (4%)
  between operations  15.3 us (2%)
    all_to_all x1, waiting for transfers between devices, spread_sum(): got = lax.all_to_all(blocks, axis, 0, 0, tiled=False)  164 us
    ppermute x4, waiting for transfers between devices, row_sum(): return mine + lax.ppermute(theirs, 'tensor', ACROSS)  106 us
    all_gather x1, waiting for transfers between devices, shards(): attn_all = lax.all_gather(attn_pack, 'dp', axis=0, tiled=True)  72.5 us
    ppermute x4, waiting for transfers between devices, row_gather(): across = lax.ppermute(values, 'tensor', ACROSS)  66.2 us
    all_gather x1, waiting for transfers between devices, shards(): mlp_all = lax.all_gather(mlp_pack, 'dp', axis=0, tiled=True)  63.5 us
    unnamed x101, local copies, waits for them, and re-layouts  40.4 us
    dot_general x8, matrix products, matmul_plain(): return jnp.dot(left, right, preferred_element_type=jnp.float32)  36.9 us
    unnamed x4, waiting for transfers between devices  31.9 us
  transfers between devices with their start and end apart: 22, of which 19 were waited for; matrix products, arithmetic and copies ran while one was open for 19% of the time, Pallas kernels for 0%

commit v1 on v0

--- a/solution.py
+++ b/solution.py
@@ -126,7 +126,9 @@
     cot_local = cotangent[0].reshape(-1, model_width)
     attn_pack = jnp.concatenate([w_query, w_forget, w_value, w_outgate, w_output.T], axis=1)
     mlp_pack = jnp.concatenate([w_gate, w_up, w_down.T], axis=1)
-    attn_all = lax.all_gather(attn_pack, "dp", axis=0, tiled=True)
+    attn_all = jnp.concatenate(
+        lax.all_to_all(jnp.stack([attn_pack] * lax.axis_size("dp")), "dp", 0, 0), axis=0
+    )
     mlp_all = lax.all_gather(mlp_pack, "dp", axis=0, tiled=True)
     wq_all = attn_all[:, 0 * local_width : 1 * local_width]
     wf_all = attn_all[:, 1 * local_width : 2 * local_width]

time: 813 us -> 841 us (1.034)
  starting transfers between devices: 34 us -> 57.9 us
    ppermute x4, waiting for transfers between devices: 66.2 us -> 168 us  [row_gather(): across = lax.ppermute(values, 'tensor', ACROSS)]
    all_gather x1 -> x0, waiting for transfers between devices: 72.5 us -> none  [shards(): attn_all = lax.all_gather(attn_pack, 'dp', axis=0, tiled=True)]
    all_gather x1, waiting for transfers between devices: 63.5 us -> 0.01 us  [shards(): mlp_all = lax.all_gather(mlp_pack, 'dp', axis=0, tiled=True)]
    all_to_all x0 -> x1, waiting for transfers between devices: none -> 34.5 us  [shards(): lax.all_to_all(jnp.stack([attn_pack] * lax.axis_size('dp')), 'dp', 0, 0)]
    all_to_all x1, starting transfers between devices: 7.17 us -> 23.6 us  [small_sum(): lax.all_to_all(jnp.swapaxes(blocks, 0, 1), ('dp', 'tensor'), 0, 0, tiled=...]
    unnamed x101 -> x97, local copies, waits for them, and re-layouts: 40.4 us -> 33.8 us
    unnamed x4 -> x3, waiting for transfers between devices: 31.9 us -> 33.2 us
  transfers between devices with their start and end apart: 22 -> 22, of which waited for: 19 -> 17; matrix products, arithmetic and copies ran while one was open for 19% -> 20% of each run, Pallas kernels for 0% -> 0%
where the time goes in v1:
time: 841 us; the launch traced here: 835 us
  waiting for transfers between devices  525 us (62%)
  matrix products  115 us (14%)
  local copies, waits for them, and re-layouts  83.8 us (10%)
  starting transfers between devices  57.9 us (7%)
  other arithmetic  37.9 us (5%)
  between operations  15.6 us (2%)
    ppermute x4, waiting for transfers between devices, row_gather(): across = lax.ppermute(values, 'tensor', ACROSS)  168 us
    all_to_all x1, waiting for transfers between devices, spread_sum(): got = lax.all_to_all(blocks, axis, 0, 0, tiled=False)  160 us
    ppermute x4, waiting for transfers between devices, row_sum(): return mine + lax.ppermute(theirs, 'tensor', ACROSS)  108 us
    dot_general x8, matrix products, matmul_plain(): return jnp.dot(left, right, preferred_element_type=jnp.float32)  36.4 us
    all_to_all x1, waiting for transfers between devices, shards(): lax.all_to_all(jnp.stack([attn_pack] * lax.axis_size('dp')), 'dp', 0, 0)  34.5 us
    unnamed x97, local copies, waits for them, and re-layouts  33.8 us
    unnamed x3, waiting for transfers between devices  33.2 us
    dot_general x8, matrix products, times_trans(): lax.dot_general(left, right, (((1,), (1,)), ((), ())), preferred_element_...  32.2 us
  transfers between devices with their start and end apart: 22, of which 17 were waited for; matrix products, arithmetic and copies ran while one was open for 20% of the time, Pallas kernels for 0%

profile of v1, /device:TPU:0, one launch (start us, length us, event | category | flops | bytes accessed | tf_op | source)
XLA Modules:
  0.0 834.8 jit_solution(5852013289236495500)
XLA Ops:
  10.8 11.1 %all-to-all-start = ((f32[128,3,16]{2,1,0:T(4,128)}), f32[128,3,16]{2,1,0:T(4,128)S(1)}, u32[]{:S(2)}, u32[]{:S(2)}) async-start(f32[128,3,16]{2,1,0:T(4,128)} %broadcast_in_dim.29), calls=%async_computation | async-start | bytes 524288 | tf_op jit(solution)/shard_map/all_to_all | solution.py:85
  22.1 10.7 %all-to-all-done = f32[128,3,16]{2,1,0:T(4,128)S(1)} async-done(((f32[128,3,16]{2,1,0:T(4,128)}), f32[128,3,16]{2,1,0:T(4,128)S(1)}, u32[]{:S(2)}, u32[]{:S(2)}) %all-to-all-start) | async-done | bytes 24608 | tf_op jit(solution)/shard_map/all_to_all | solution.py:85
  32.8 5.2 stack.44
  38.0 5.2 all-to-all-start.1
  45.6 134.0 %collective-permute-done = bf16[128,2048]{1,0:T(8,128)(2,1)S(1)} collective-permute-done((bf16[128,2048]{1,0:T(8,128)(2,1)S(1)}, bf16[128,2048]{1,0:T(8,128)(2,1)S(1)}, u32[]{:S(2)}, u32[]{:S(2)}) %collective-permute-start) | collective-permute-done | bytes 524320 | tf_op jit(solution)/shard_map/ppermute | solution.py:62
  185.4 34.5 %all-to-all-done.1 = bf16[32,64,2560]{2,1,0:T(8,128)(2,1)} async-done(((bf16[32,64,2560]{2,1,0:T(8,128)(2,1)}), bf16[32,64,2560]{2,1,0:T(8,128)(2,1)}, u32[]{:S(2)}, u32[]{:S(2)}) %all-to-all-start.1) | async-done | bytes 10485792 | tf_op jit(solution)/shard_map/all_to_all | solution.py:130
  219.9 5.4 slice_bitcast_fusion
  225.3 4.1 copy.76
  229.4 4.0 copy.78
  235.8 3.6 fusion.56
  253.5 4.9 fusion.74
  258.4 3.1 fusion.29
  261.8 4.1 collective-permute-done.2
  266.1 3.2 collective-permute-start.3
  270.6 24.6 %collective-permute-done.3 = f32[128,2048]{1,0:T(8,128)} collective-permute-done((f32[128,2048]{1,0:T(8,128)S(1)}, f32[128,2048]{1,0:T(8,128)}, u32[]{:S(2)}, u32[]{:S(2)}) %collective-permute-start.3) | collective-permute-done | bytes 1048608 | tf_op jit(solution)/shard_map/ppermute | solution.py:73
  298.1 8.2 collective-permute-done.8
  307.8 9.6 %collective-permute-done.4 = bf16[128,2048]{1,0:T(8,128)(2,1)S(1)} collective-permute-done((bf16[128,2048]{1,0:T(8,128)(2,1)S(1)}, bf16[128,2048]{1,0:T(8,128)(2,1)S(1)}, u32[]{:S(2)}, u32[]{:S(2)}) %collective-permute-start.4) | collective-permute-done | bytes 524320 | tf_op jit(solution)/shard_map/ppermute | solution.py:62
  321.8 7.0 fusion
  330.7 3.4 fusion.6
  334.1 7.3 multiply_convert_fusion.1
  341.5 3.5 convolution_convert_fusion
  345.0 3.5 convolution_convert_fusion.1
  348.4 3.5 convolution_convert_fusion.2
  351.9 7.8 pad_maximum_fusion
  359.7 21.0 %copy.104 = bf16[2048,4224]{1,0:T(8,128)(2,1)} copy(bf16[2048,4224]{0,1:T(8,128)(2,1)} %pad_maximum_fusion) | data formatting | bytes 34603008
  380.8 6.0 fusion.4
  386.8 5.5 fusion.12
  393.7 5.5 fusion.2
  400.4 3.3 collective-permute-done.6
  404.2 29.6 %collective-permute-done.11 = f32[128,2048]{1,0:T(8,128)S(1)} collective-permute-done((f32[128,2048]{1,0:T(8,128)S(1)}, f32[128,2048]{1,0:T(8,128)S(1)}, u32[]{:S(2)}, u32[]{:S(2)}) %collective-permute-start.11) | collective-permute-done | bytes 1048608 | tf_op jit(solution)/shard_map/ppermute | solution.py:73
  434.3 28.8 %collective-permute-done.7 = f32[128,2048]{1,0:T(8,128)S(1)} collective-permute-done((f32[128,2048]{1,0:T(8,128)S(1)}, f32[128,2048]{1,0:T(8,128)S(1)}, u32[]{:S(2)}, u32[]{:S(2)}) %collective-permute-start.7) | collective-permute-done | bytes 1048608 | tf_op jit(solution)/shard_map/ppermute | solution.py:73
  464.8 16.0 %collective-permute-done.12 = bf16[128,2048]{1,0:T(8,128)(2,1)S(1)} collective-permute-done((bf16[128,2048]{1,0:T(8,128)(2,1)S(1)}, bf16[128,2048]{1,0:T(8,128)(2,1)S(1)}, u32[]{:S(2)}, u32[]{:S(2)}) %collective-permute-start.12) | collective-permute-done | bytes 524320 | tf_op jit(solution)/shard_map/ppermute | solution.py:62
  484.0 4.7 fusion.76
  491.7 3.2 fusion.59
  496.2 3.3 convolution_select_fusion
  508.8 2.9 fusion.36
  511.8 3.0 fusion.34
  514.8 3.1 add_add_fusion
  520.9 4.3 fusion.19
  528.5 4.4 fusion.18
  538.3 24.5 %collective-permute-done.15 = f32[128,2048]{1,0:T(8,128)} collective-permute-done((f32[128,2048]{1,0:T(8,128)S(1)}, f32[128,2048]{1,0:T(8,128)}, u32[]{:S(2)}, u32[]{:S(2)}) %collective-permute-start.15) | collective-permute-done | bytes 1048608 | tf_op jit(solution)/shard_map/ppermute | solution.py:73
  566.1 23.6 %all-to-all-start.2 = ((f32[128,3,16]{2,1,0:T(4,128)}), f32[128,3,16]{2,1,0:T(4,128)S(1)}, u32[]{:S(2)}, u32[]{:S(2)}) async-start(f32[128,3,16]{2,1,0:T(4,128)} %copy.89), calls=%async_computation.2 | async-start | bytes 524288 | tf_op jit(solution)/shard_map/all_to_all | solution.py:92
  589.7 4.2 fusion.15
  593.9 13.8 %copy.90 = bf16[2048,2560]{1,0:T(8,128)(2,1)} copy(bf16[2048,2560]{0,1:T(8,128)(2,1)} %fusion.15) | data formatting | bytes 20971520 | tf_op jit(solution)/shard_map/concatenate | solution.py:208
  607.7 9.7 %all-to-all-start.3 = ((bf16[32,64,2560]{2,1,0:T(8,128)(2,1)}), bf16[32,64,2560]{2,1,0:T(8,128)(2,1)}, u32[]{:S(2)}, u32[]{:S(2)}) async-start(bf16[32,64,2560]{2,1,0:T(8,128)(2,1)} %bitcast.266), calls=%async_computation.3 | async-start | bytes 20971520 | tf_op jit(solution)/shard_map/all_to_all | solution.py:78
  619.4 159.8 %all-to-all-done.3 = bf16[32,64,2560]{2,1,0:T(8,128)(2,1)} async-done(((bf16[32,64,2560]{2,1,0:T(8,128)(2,1)}), bf16[32,64,2560]{2,1,0:T(8,128)(2,1)}, u32[]{:S(2)}, u32[]{:S(2)}) %all-to-all-start.3) | async-done | bytes 10485792 | tf_op jit(solution)/shard_map/all_to_all | solution.py:78
  779.2 5.8 convert_reduce_fusion
  785.9 33.1 %reduce-scatter.4.cloned.1.call-done = bf16[64,4224]{1,0:T(8,128)(2,1)} async-done(((bf16[2048,4224]{1,0:T(8,128)(2,1)}), bf16[64,4224]{1,0:T(8,128)(2,1)}) %reduce-scatter.4.cloned.1.call-update) | async-done | bytes 540688
  (205 shorter events, 88.5 us)
Async XLA Ops:
  7.2 172.7 %copy-start = (s32[1,4,128]{2,1,0:T(4,128)S(1)}, s32[1,4,128]{2,1,0:T(4,128)}, u32[]{:S(2)}) copy-start(s32[1,4,128]{2,1,0:T(4,128)} %param.16) | copy-start | bytes 6148
  7.2 14.8 %copy-start.28 = (bf16[64,512]{1,0:T(8,128)(2,1)S(1)}, bf16[64,512]{1,0:T(8,128)(2,1)}, u32[]{:S(2)}) copy-start(bf16[64,512]{1,0:T(8,128)(2,1)} %param.19) | copy-start | bytes 196612
  7.2 14.8 %copy-start.29 = (bf16[64,512]{1,0:T(8,128)(2,1)S(1)}, bf16[64,512]{1,0:T(8,128)(2,1)}, u32[]{:S(2)}) copy-start(bf16[64,512]{1,0:T(8,128)(2,1)} %param.20) | copy-start | bytes 196612
  7.2 14.8 %copy-start.30 = (bf16[64,512]{1,0:T(8,128)(2,1)S(1)}, bf16[64,512]{1,0:T(8,128)(2,1)}, u32[]{:S(2)}) copy-start(bf16[64,512]{1,0:T(8,128)(2,1)} %param.21) | copy-start | bytes 196612
  7.2 14.8 %copy-start.31 = (bf16[64,512]{1,0:T(8,128)(2,1)S(1)}, bf16[64,512]{1,0:T(8,128)(2,1)}, u32[]{:S(2)}) copy-start(bf16[64,512]{1,0:T(8,128)(2,1)} %param.22) | copy-start | bytes 196612
  7.2 14.8 %copy-start.32 = (bf16[512,64]{0,1:T(8,128)(2,1)S(1)}, bf16[512,64]{0,1:T(8,128)(2,1)}, u32[]{:S(2)}) copy-start(bf16[512,64]{0,1:T(8,128)(2,1)} %param.23) | copy-start | bytes 196612
  7.2 314.5 %all-gather.2.cloned.1.call-start = ((), (), s32[]{:S(2)}) async-start(), calls=%async_computation.5 | async-start | bytes 17842176 | tf_op jit(solution)/shard_map/all_gather | solution.py:132
  10.8 22.0 %all-to-all-start = ((f32[128,3,16]{2,1,0:T(4,128)}), f32[128,3,16]{2,1,0:T(4,128)S(1)}, u32[]{:S(2)}, u32[]{:S(2)}) async-start(f32[128,3,16]{2,1,0:T(4,128)} %broadcast_in_dim.29), calls=%async_computation | async-start | bytes 524288 | tf_op jit(solution)/shard_map/all_to_all | solution.py:85
  38.0 5.2 copy-start.3
  38.0 181.9 %all-to-all-start.1 = ((bf16[32,64,2560]{2,1,0:T(8,128)(2,1)}), bf16[32,64,2560]{2,1,0:T(8,128)(2,1)}, u32[]{:S(2)}, u32[]{:S(2)}) async-start(bf16[32,64,2560]{2,1,0:T(8,128)(2,1)} %stack.44), calls=%async_computation.1 | async-start | bytes 20971520 | tf_op jit(solution)/shard_map/all_to_all | solution.py:130
  43.2 775.9 %reduce-scatter.4.cloned.1.call-start = ((), (), s32[]{:S(2)}) async-start(), calls=%async_computation.6 | async-start | bytes 17842176
  43.9 135.7 %copy-start.33 = (f32[128]{0:T(128)}, f32[128]{0:T(128)S(1)}, u32[]{:S(2)}) copy-start(f32[128]{0:T(128)S(1)} %get-tuple-element.105) | copy-start | bytes 1540
  44.6 135.1 %copy-start.26 = (f32[2048]{0:T(1024)}, f32[2048]{0:T(1024)S(1)}, u32[]{:S(2)}) copy-start(f32[2048]{0:T(1024)S(1)} %mul.250) | copy-start | bytes 24580
  44.6 135.2 %copy-start.36 = (s32[4]{0:T(128)S(1)}, s32[4]{0:T(128)}, u32[]{:S(2)}) copy-start(s32[4]{0:T(128)} %constant.52.clone) | copy-start | bytes 52
  44.8 134.8 %collective-permute-start = (bf16[128,2048]{1,0:T(8,128)(2,1)S(1)}, bf16[128,2048]{1,0:T(8,128)(2,1)S(1)}, u32[]{:S(2)}, u32[]{:S(2)}) collective-permute-start(bf16[128,2048]{1,0:T(8,128)(2,1)S(1)} %fusion.62), channel_id=1, source_target_pairs={{0,2},{2,0},{1,3},{3,1},{4,6},{6,4},{5,7},{7,5},{8,10},{10,8},{9,1... | collective-permute-start | bytes 1572872 | tf_op jit(solution)/shard_map/ppermute | solution.py:62
  179.6 5.8 copy-start.20
  179.7 2.9 collective-permute-start.1
  235.8 4.6 copy-start.21
  239.4 4.5 copy-start.6
  261.7 7.6 copy-start.8
  261.7 4.2 collective-permute-start.2
  266.1 29.0 %collective-permute-start.3 = (f32[128,2048]{1,0:T(8,128)S(1)}, f32[128,2048]{1,0:T(8,128)}, u32[]{:S(2)}, u32[]{:S(2)}) collective-permute-start(f32[128,2048]{1,0:T(8,128)S(1)} %fusion.88), channel_id=1, source_target_pairs={{0,2},{2,0},{1,3},{3,1},{4,6},{6,4},{5,7},{7,5},{8,10},{10,8},{9,1... | collective-permute-start | bytes 3145736 | tf_op jit(solution)/shard_map/ppermute | solution.py:73
  269.4 37.0 %collective-permute-start.8 = (bf16[128,2048]{1,0:T(8,128)(2,1)S(1)}, bf16[128,2048]{1,0:T(8,128)(2,1)}, u32[]{:S(2)}, u32[]{:S(2)}) collective-permute-start(bf16[128,2048]{1,0:T(8,128)(2,1)S(1)} %bitcast.267), channel_id=1, source_target_pairs={{0,2},{2,0},{1,3},{3,1},{4,6},{6,4},{5,7},{7,5},{8,10},{10,8},{9,1... | collective-permute-start | bytes 1572872 | tf_op jit(solution)/shard_map/ppermute | solution.py:62
  297.6 19.7 %collective-permute-start.4 = (bf16[128,2048]{1,0:T(8,128)(2,1)S(1)}, bf16[128,2048]{1,0:T(8,128)(2,1)S(1)}, u32[]{:S(2)}, u32[]{:S(2)}) collective-permute-start(bf16[128,2048]{1,0:T(8,128)(2,1)S(1)} %multiply_convert_fusion.4), channel_id=1, source_target_pairs={{0,2},{2,0},{1,3},{3,1},{4,6},{6,4},{5,7},{7,5},{8,10},{10,8},{9,1... | collective-permute-start | bytes 1572872 | tf_op jit(solution)/shard_map/ppermute | solution.py:62
  307.5 10.0 %collective-permute-start.9 = (bf16[2,128,2048]{2,1,0:T(8,128)(2,1)S(1)}, bf16[2,128,2048]{2,1,0:T(8,128)(2,1)S(1)}, u32[]{:S(2)}, u32[]{:S(2)}) collective-permute-start(bf16[2,128,2048]{2,1,0:T(8,128)(2,1)S(1)} %pad_maximum_fusion.7), channel_id=1, source_target_pairs={{0,1},{1,0},{2,3},{3,2},{4,5},{5,4},{6,7},{7,6},{8,9},{9,8},{10,11... | collective-permute-start | bytes 3145736 | tf_op jit(solution)/shard_map/ppermute | solution.py:64
  317.4 2.7 collective-permute-start.5
  321.8 7.0 copy-start.17
  321.8 8.9 %copy-start.37 = (bf16[2048,4224]{1,0:T(8,128)(2,1)S(1)}, bf16[2048,4224]{1,0:T(8,128)(2,1)}, u32[]{:S(2)}) copy-start(bf16[2048,4224]{1,0:T(8,128)(2,1)} %all-gather.2.cloned.1.call-done) | copy-start | bytes 51904516
  334.1 7.4 copy-start.16
  341.5 7.0 copy-start.38
  380.8 6.1 copy-start.39
  392.6 7.3 collective-permute-start.10
  399.4 4.3 collective-permute-start.6
  400.0 33.8 %collective-permute-start.11 = (f32[128,2048]{1,0:T(8,128)S(1)}, f32[128,2048]{1,0:T(8,128)S(1)}, u32[]{:S(2)}, u32[]{:S(2)}) collective-permute-start(f32[128,2048]{1,0:T(8,128)S(1)} %fusion.80), channel_id=1, source_target_pairs={{0,2},{2,0},{1,3},{3,1},{4,6},{6,4},{5,7},{7,5},{8,10},{10,8},{9,1... | collective-permute-start | bytes 3145736 | tf_op jit(solution)/shard_map/ppermute | solution.py:73
  403.8 59.3 %collective-permute-start.7 = (f32[128,2048]{1,0:T(8,128)S(1)}, f32[128,2048]{1,0:T(8,128)S(1)}, u32[]{:S(2)}, u32[]{:S(2)}) collective-permute-start(f32[128,2048]{1,0:T(8,128)S(1)} %fusion.83), channel_id=1, source_target_pairs={{0,2},{2,0},{1,3},{3,1},{4,6},{6,4},{5,7},{7,5},{8,10},{10,8},{9,1... | collective-permute-start | bytes 3145736 | tf_op jit(solution)/shard_map/ppermute | solution.py:73
  464.8 16.0 %collective-permute-start.12 = (bf16[128,2048]{1,0:T(8,128)(2,1)S(1)}, bf16[128,2048]{1,0:T(8,128)(2,1)S(1)}, u32[]{:S(2)}, u32[]{:S(2)}) collective-permute-start(bf16[128,2048]{1,0:T(8,128)(2,1)S(1)} %get-tuple-element.75), channel_id=1, source_target_pairs={{0,2},{2,0},{1,3},{3,1},{4,6},{6,4},{5,7},{7,5},{8,10},{10,8},{9,1... | collective-permute-start | bytes 1572872 | tf_op jit(solution)/shard_map/ppermute | solution.py:62
  480.9 3.0 collective-permute-start.13
  484.0 4.8 copy-start.15
  520.7 4.5 collective-permute-start.14
  526.9 35.9 %collective-permute-start.15 = (f32[128,2048]{1,0:T(8,128)S(1)}, f32[128,2048]{1,0:T(8,128)}, u32[]{:S(2)}, u32[]{:S(2)}) collective-permute-start(f32[128,2048]{1,0:T(8,128)S(1)} %fusion.77), channel_id=1, source_target_pairs={{0,2},{2,0},{1,3},{3,1},{4,6},{6,4},{5,7},{7,5},{8,10},{10,8},{9,1... | collective-permute-start | bytes 3145736 | tf_op jit(solution)/shard_map/ppermute | solution.py:73
  535.6 27.3 %copy-start.27 = (f32[2048]{0:T(1024)S(1)}, f32[2048]{0:T(1024)}, u32[]{:S(2)}) copy-start(f32[2048]{0:T(1024)} %copy-done.26) | copy-start | bytes 24580
  535.6 27.3 %copy-start.34 = (f32[128]{0:T(128)S(1)}, f32[128]{0:T(128)}, u32[]{:S(2)}) copy-start(f32[128]{0:T(128)} %copy-done.33) | copy-start | bytes 1540
  538.3 51.4 %copy-start.23 = (bf16[512,512]{1,0:T(8,128)(2,1)S(1)}, bf16[512,512]{1,0:T(8,128)(2,1)}, u32[]{:S(2)}) copy-start(bf16[512,512]{1,0:T(8,128)(2,1)} %copy-done.22) | copy-start | bytes 1572868
  566.1 41.6 %all-to-all-start.2 = ((f32[128,3,16]{2,1,0:T(4,128)}), f32[128,3,16]{2,1,0:T(4,128)S(1)}, u32[]{:S(2)}, u32[]{:S(2)}) async-start(f32[128,3,16]{2,1,0:T(4,128)} %copy.89), calls=%async_computation.2 | async-start | bytes 524288 | tf_op jit(solution)/shard_map/all_to_all | solution.py:92
  607.7 9.7 %copy-start.10 = (f32[128,2048]{1,0:T(8,128)S(1)}, f32[128,2048]{1,0:T(8,128)}, u32[]{:S(2)}) copy-start(f32[128,2048]{1,0:T(8,128)} %get-tuple-element.76) | copy-start | bytes 3145732
  607.7 9.7 %copy-start.35 = (f32[128]{0:T(128)S(1)}, f32[128]{0:T(128)}, u32[]{:S(2)}) copy-start(f32[128]{0:T(128)} %get-tuple-element.104) | copy-start | bytes 1540
  607.7 171.5 %all-to-all-start.3 = ((bf16[32,64,2560]{2,1,0:T(8,128)(2,1)}), bf16[32,64,2560]{2,1,0:T(8,128)(2,1)}, u32[]{:S(2)}, u32[]{:S(2)}) async-start(bf16[32,64,2560]{2,1,0:T(8,128)(2,1)} %bitcast.266), calls=%async_computation.3 | async-start | bytes 20971520 | tf_op jit(solution)/shard_map/all_to_all | solution.py:78
  822.2 5.3 copy-start.1
  (18 other events, 52.0 us)
Sparse Core Ops, SparseCore 0:
  11.1 288.4 all-gather.1
  380.9 438.1 reduce-scatter.3
